TPU v7x, 32 devices: a whole 2x2x4 slice. The times are simulated.
32 devices in a mesh: dp: 8 (over y, x, core), mem: 4 (over z).
Axes of the slice: x: 2, y: 2, z: 4, core: 2. Of those that a mesh axis runs over, the one named last changes fastest.
Arguments:
- inputs: bfloat16 [32, 100, 768], P('dp'), may hold values from -6 to 6
- memory: bfloat16 [32, 1280, 768], P('dp', 'mem'), may hold values from -6 to 6
- lengths: int32 [32], P('dp'), may hold values from 1 to 1280, as said below
- self_query: bfloat16 [768, 768], P('dp'), may hold values from -0.21875 to 0.21875
- self_key: bfloat16 [768, 768], P('dp'), may hold values from -0.21875 to 0.21875
- self_value: bfloat16 [768, 768], P('dp'), may hold values from -0.21875 to 0.21875
- self_out: bfloat16 [768, 768], P('dp'), may hold values from -0.625 to 0.625
- cross_query: bfloat16 [768, 768], P('dp'), may hold values from -0.21875 to 0.21875
- cross_key: bfloat16 [768, 768], P('dp'), may hold values from -0.21875 to 0.21875
- cross_value: bfloat16 [768, 768], P('dp'), may hold values from -0.21875 to 0.21875
- cross_out: bfloat16 [768, 768], P('dp'), may hold values from -1 to 1
- expand_weight: bfloat16 [768, 3072], P('dp'), may hold values from -0.21875 to 0.21875
- contract_weight: bfloat16 [3072, 768], P('dp'), may hold values from -0.109375 to 0.109375
- gain_one: float32 [768], replicated, may hold values from 0.5 to 1.5
- shift_one: float32 [768], replicated, may hold values from -1.5 to 1.5
- gain_two: float32 [768], replicated, may hold values from 0.5 to 1.5
- shift_two: float32 [768], replicated, may hold values from -1.5 to 1.5
- gain_three: float32 [768], replicated, may hold values from 0.5 to 1.5
- shift_three: float32 [768], replicated, may hold values from -1.5 to 1.5
- cotangent: bfloat16 [32, 100, 768], P('dp'), may hold values from -6 to 6
Outputs:
- output: float32 [32, 100, 768], P('dp')
- input_grad: float32 [32, 100, 768], P('dp')
- memory_grad: float32 [32, 1280, 768], P('dp', 'mem')
- self_query_grad: float32 [768, 768], P('dp')
- self_key_grad: float32 [768, 768], P('dp')
- self_value_grad: float32 [768, 768], P('dp')
- self_out_grad: float32 [768, 768], P('dp')
- cross_query_grad: float32 [768, 768], P('dp')
- cross_key_grad: float32 [768, 768], P(('dp', 'mem'))
- cross_value_grad: float32 [768, 768], P(('dp', 'mem'))
- cross_out_grad: float32 [768, 768], P('dp')
- expand_grad: float32 [768, 3072], P('dp')
- contract_grad: float32 [3072, 768], P('dp')
- gain_one_grad: float32 [768], P('dp')
- shift_one_grad: float32 [768], P('dp')
- gain_two_grad: float32 [768], P('dp')
- shift_two_grad: float32 [768], P('dp')
- gain_three_grad: float32 [768], P('dp')
- shift_three_grad: float32 [768], P('dp')
Inputs may be any that keep to these rules, and one draw needn't show every extreme that they name: `lengths`: the number of valid memory tokens of each image; in each aligned block of 4 images one image has all 1280.
All inputs are finite; a program needn't handle non-finite values.
Results may differ from a plain program's by a relative error of at most 0.023.
Values may be sent and summed in bfloat16 or wider, within the bound.
A program may use at most 320 MiB of HBM per device.

v0:
```python
import jax
import jax.numpy as jnp
from jax import lax
from jax.sharding import PartitionSpec as P

H = 12
LOW = jnp.bfloat16
WIDE = jnp.float32


def mm(a, b, dims):
    return lax.dot_general(a, b, (dims, ((), ())), preferred_element_type=WIDE)


def project(values, weight):
    return mm(values, weight, ((1,), (0,)))


def back_project(grads, weight):
    return mm(grads, weight, ((1,), (1,)))


def weight_grad(left, right):
    return mm(left, right, ((0,), (0,)))


def heads_of(values, images):
    rows, width = values.shape
    return values.reshape(images, rows // images, H, width // H)


def norm_forward(resid, gain, shift):
    center = resid - jnp.mean(resid, axis=-1, keepdims=True)
    inverse = lax.rsqrt(jnp.mean(center * center, axis=-1, keepdims=True) + 1e-05)
    normed = center * inverse
    return (normed * gain + shift, normed, inverse)


def norm_backward(incoming, normed, inverse, gain):
    scaled = incoming * gain
    grad_in = inverse * (
        scaled
        - jnp.mean(scaled, axis=-1, keepdims=True)
        - normed * jnp.mean(scaled * normed, axis=-1, keepdims=True)
    )
    return (grad_in, jnp.sum(incoming * normed, axis=0), jnp.sum(incoming, axis=0))


def scores_of(query, keys):
    return jnp.einsum("bqhe,bkhe->bhqk", query, keys, preferred_element_type=WIDE) * 0.125


def mix(probs, values):
    return jnp.einsum("bhqk,bkhe->bqhe", probs, values, preferred_element_type=WIDE)


def mix_back(probs, grads):
    return jnp.einsum("bhqk,bqhe->bkhe", probs, grads, preferred_element_type=WIDE)


def attention_backward(probs, attn, grad_attn, query, keys, values):
    row = jnp.sum(grad_attn.astype(WIDE) * attn.astype(WIDE), axis=-1).transpose(0, 2, 1)[..., None]
    grad_probs = jnp.einsum("bqhe,bkhe->bhqk", grad_attn, values, preferred_element_type=WIDE)
    grad_scores = (probs * (grad_probs - row)).astype(LOW)
    grad_query = mix(grad_scores, keys) * 0.125
    grad_keys = mix_back(grad_scores, query) * 0.125
    grad_values = mix_back(probs.astype(LOW), grad_attn)
    return (grad_query, grad_keys, grad_values)


def gelu_tanh(values):
    return jax.nn.gelu(values, approximate=True)


def on_device(
    inputs,
    memory,
    lengths,
    self_query,
    self_key,
    self_value,
    self_out,
    cross_query,
    cross_key,
    cross_value,
    cross_out,
    expand_weight,
    contract_weight,
    gain_one,
    shift_one,
    gain_two,
    shift_two,
    gain_three,
    shift_three,
    cotangent,
):
    images, queries, width = inputs.shape
    mem_rows = memory.shape[1]
    rows = images * queries
    share = self_query.shape[0]
    parts = width // share
    squares = (
        self_query,
        self_key,
        self_value,
        self_out,
        cross_query,
        cross_key,
        cross_value,
        cross_out,
    )
    packed = lax.all_gather(jnp.stack(squares), "dp", axis=1, tiled=True)
    expand_full = lax.all_gather(expand_weight, "dp", axis=0, tiled=True)
    contract_full = lax.all_gather(contract_weight, "dp", axis=0, tiled=True)
    query_full, key_full, value_full, out_full, cquery_full, ckey_full, cvalue_full, cout_full = (
        packed
    )
    tokens = inputs.reshape(rows, width)
    memory_flat = memory.reshape(images * mem_rows, width)
    incoming = cotangent.reshape(rows, width).astype(WIDE)

    def joined(values):
        return values.reshape(-1, width)

    query_heads = heads_of(project(tokens, query_full).astype(LOW), images)
    key_heads = heads_of(project(tokens, key_full).astype(LOW), images)
    value_heads = heads_of(project(tokens, value_full).astype(LOW), images)
    self_raw = scores_of(query_heads, key_heads)
    self_exp = jnp.exp(self_raw - jnp.max(self_raw, axis=-1, keepdims=True))
    self_probs = self_exp / jnp.sum(self_exp, axis=-1, keepdims=True)
    self_attn = joined(mix(self_probs.astype(LOW), value_heads)).astype(LOW)
    first, normed_one, inverse_one = norm_forward(
        tokens.astype(WIDE) + project(self_attn, out_full), gain_one, shift_one
    )
    first_low = first.astype(LOW)
    cross_q = heads_of(project(first_low, cquery_full).astype(LOW), images)
    cross_k = heads_of(project(memory_flat, ckey_full).astype(LOW), images)
    cross_v = heads_of(project(memory_flat, cvalue_full).astype(LOW), images)
    places = lax.axis_index("mem") * mem_rows + jnp.arange(mem_rows, dtype=jnp.int32)
    valid = (places[None, :] < lengths[:, None])[:, None, None, :]
    cross_raw = jnp.where(valid, scores_of(cross_q, cross_k), -1e30)
    top = lax.pmax(jnp.max(cross_raw, axis=-1, keepdims=True), "mem")
    cross_exp = jnp.where(valid, jnp.exp(cross_raw - top), 0.0)
    total = lax.psum(jnp.sum(cross_exp, axis=-1, keepdims=True), "mem")
    cross_probs = cross_exp / total
    cross_attn = lax.psum(joined(mix(cross_probs.astype(LOW), cross_v)).astype(LOW), "mem")
    second, normed_two, inverse_two = norm_forward(
        first + project(cross_attn, cout_full), gain_two, shift_two
    )
    second_low = second.astype(LOW)
    pre_act = project(second_low, expand_full)
    activ, gelu_pull = jax.vjp(gelu_tanh, pre_act)
    activ_low = activ.astype(LOW)
    result, normed_three, inverse_three = norm_forward(
        second + project(activ_low, contract_full), gain_three, shift_three
    )
    grad_three, gain_three_part, shift_three_part = norm_backward(
        incoming, normed_three, inverse_three, gain_three
    )
    grad_ffn = grad_three.astype(LOW)

    def scattered(part, axes="dp"):
        return lax.psum_scatter(part, axes, scatter_dimension=0, tiled=True).astype(WIDE)

    contract_grad = scattered(weight_grad(activ_low, grad_ffn).astype(LOW))
    grad_pre = gelu_pull(back_project(grad_ffn, contract_full))[0].astype(LOW)
    expand_grad = scattered(weight_grad(second_low, grad_pre).astype(LOW))
    grad_second = grad_three + back_project(grad_pre, expand_full)
    grad_two, gain_two_part, shift_two_part = norm_backward(
        grad_second, normed_two, inverse_two, gain_two
    )
    grad_cross = grad_two.astype(LOW)
    cout_part = weight_grad(cross_attn, grad_cross)
    grad_cattn = heads_of(back_project(grad_cross, cout_full).astype(LOW), images)
    part_cquery, grad_ckey, grad_cvalue = attention_backward(
        cross_probs, heads_of(cross_attn, images), grad_cattn, cross_q, cross_k, cross_v
    )
    grad_cquery = lax.psum(joined(part_cquery).astype(LOW), "mem")
    grad_ckey = joined(grad_ckey).astype(LOW)
    grad_cvalue = joined(grad_cvalue).astype(LOW)
    kv_grad = scattered(
        jnp.concatenate(
            [weight_grad(memory_flat, grad_ckey), weight_grad(memory_flat, grad_cvalue)], axis=1
        ).astype(LOW),
        ("dp", "mem"),
    )
    memory_grad = back_project(grad_ckey, ckey_full) + back_project(grad_cvalue, cvalue_full)
    cquery_part = weight_grad(first_low, grad_cquery)
    grad_first = grad_two + back_project(grad_cquery, cquery_full)
    grad_one, gain_one_part, shift_one_part = norm_backward(
        grad_first, normed_one, inverse_one, gain_one
    )
    grad_self = grad_one.astype(LOW)
    out_part = weight_grad(self_attn, grad_self)
    grad_sattn = heads_of(back_project(grad_self, out_full).astype(LOW), images)
    grad_query, grad_key, grad_value = (
        joined(grad).astype(LOW)
        for grad in attention_backward(
            self_probs, heads_of(self_attn, images), grad_sattn, query_heads, key_heads, value_heads
        )
    )
    input_grad = (
        grad_one
        + back_project(grad_query, query_full)
        + back_project(grad_key, key_full)
        + back_project(grad_value, value_full)
    )
    norm_parts = jnp.stack(
        [
            gain_one_part,
            shift_one_part,
            gain_two_part,
            shift_two_part,
            gain_three_part,
            shift_three_part,
        ],
        axis=1,
    )
    rest = scattered(
        jnp.concatenate(
            [
                weight_grad(tokens, grad_query),
                weight_grad(tokens, grad_key),
                weight_grad(tokens, grad_value),
                out_part,
                cquery_part,
                cout_part,
                jnp.pad(norm_parts, ((0, 0), (0, 122))),
            ],
            axis=1,
        ).astype(LOW)
    )
    squares_grad = [rest[:, place * width : (place + 1) * width] for place in range(6)]
    norms_grad = [rest[:, 6 * width + place] for place in range(6)]
    return (
        result.reshape(inputs.shape),
        input_grad.reshape(inputs.shape),
        memory_grad.reshape(memory.shape),
        *squares_grad[:5],
        kv_grad[:, :width],
        kv_grad[:, width:],
        squares_grad[5],
        expand_grad,
        contract_grad,
        *norms_grad,
    )


def solution(mesh):
    rows = P("dp", None)
    image = P("dp", None, None)
    token = P("dp", "mem", None)
    both = P(("dp", "mem"), None)
    return jax.shard_map(
        on_device,
        mesh=mesh,
        in_specs=(image, token, P("dp"), *[rows] * 10, *[P()] * 6, image),
        out_specs=(image, image, token, *[rows] * 5, both, both, *[rows] * 3, *[P("dp")] * 6),
        check_vma=False,
    )
```

profile of v0, /device:TPU:0, one launch (start us, length us, event | category | flops | bytes accessed | tf_op | source)
XLA Modules:
  0.0 718.2 jit_solution(10065242548972240690)
XLA Ops:
  16.4 60.3 %all-gather.4.cloned.1.call-done = bf16[8,768,768]{2,1,0:T(8,128)(2,1)} async-done(((bf16[8,96,768]{2,1,0:T(8,128)(2,1)}), bf16[8,768,768]{2,1,0:T(8,128)(2,1)}) %all-gather.4.cloned.1.call-update) | async-done | bytes 9437200 | tf_op jit(solution)/shard_map/all_gather | solution.py:112
  81.0 5.3 reshape.218
  129.7 5.1 reshape.220
  134.8 6.5 fusion.1
  141.3 19.0 %pmax.7 = f32[4,12,100]{2,1,0:T(8,128)S(1)} all-reduce(f32[4,12,100]{2,1,0:T(8,128)S(1)} %get-tuple-element.144), channel_id=1, replica_groups=mesh['dp'=8,'mem'=4] {'mem'}, use_global_device_ids=true, to_apply=%region_5.6 | all-reduce | flops 4800 | bytes 38400 | tf_op jit(solution)/shard_map/pmax | solution.py:142
  164.7 15.9 %psum.21 = f32[4,12,100]{2,1,0:T(8,128)S(1)} all-reduce(f32[4,12,100]{2,1,0:T(8,128)S(1)} %fusion.3), channel_id=1, replica_groups=mesh['dp'=8,'mem'=4] {'mem'}, use_global_device_ids=true, to_apply=%region_7.8 | all-reduce | flops 4800 | bytes 38400 | tf_op jit(solution)/shard_map/psum | solution.py:144
  180.6 5.3 fusion.44
  196.0 36.2 %all-reduce.4.cloned.1.call-done = bf16[400,768]{0,1:T(8,128)(2,1)} async-done(((bf16[400,768]{0,1:T(8,128)(2,1)}), bf16[400,768]{0,1:T(8,128)(2,1)}) %all-reduce.4.cloned.1.call-update) | async-done | bytes 614416 | tf_op jit(solution)/shard_map/psum | solution.py:146
  236.2 36.1 %all-gather.6.cloned.1.call-done = bf16[768,3072]{1,0:T(8,128)(2,1)} async-done(((bf16[96,3072]{1,0:T(8,128)(2,1)}), bf16[768,3072]{1,0:T(8,128)(2,1)}) %all-gather.6.cloned.1.call-update) | async-done | bytes 4718608 | tf_op jit(solution)/shard_map/all_gather | solution.py:113
  272.3 7.2 fusion.79
  279.5 33.5 %all-gather.8.cloned.1.call-done = bf16[3072,768]{1,0:T(8,128)(2,1)} async-done(((bf16[384,768]{1,0:T(8,128)(2,1)}), bf16[3072,768]{1,0:T(8,128)(2,1)}) %all-gather.8.cloned.1.call-update) | async-done | bytes 4718608 | tf_op jit(solution)/shard_map/all_gather | solution.py:114
  313.0 7.3 %fusion.92 = (f32[400]{0:T(512)S(1)}, f32[400,768]{1,0:T(8,128)S(1)}) fusion(bf16[3072,768]{1,0:T(8,128)(2,1)} %all-gather.8.cloned.1.call-done, f32[400,3072]{1,0:T(8,128)} %fusion.79, f32[768]{0:T(1024)S(1)} %copy-done.43, f32[768]{0:T(1024)S(1)} %copy-done.38, f32[400]{0:T(512)S(1)} %add_rsqrt_fusion.1, f32[400,768]{1,0:T(8,128)} %copy-done.10, ...), kind=kOutput, calls=%fused_computation.172 | convolution fusion | flops 1900338816 | bytes 12102336 | tf_op jit(solution)/shard_map/dot_general | solution.py:12
  324.4 4.9 fusion.10
  346.7 6.6 multiply_convert_fusion
  364.6 4.9 copy.254
  374.2 4.9 copy.256
  395.0 7.0 convolution_convert_fusion.1
  402.3 8.0 %convolution_convert_fusion = bf16[3072,768]{1,0:T(8,128)(2,1)} fusion(f32[400,768]{1,0:T(8,128)} %copy-done.29, f32[400,3072]{1,0:T(8,128)} %fusion.79), kind=kOutput, calls=%fused_computation.9 | convolution fusion | flops 1901162496 | bytes 10862592 | tf_op jit(solution)/shard_map/dot_general | solution.py:12
  461.2 10.1 %copy.272 = bf16[768,4736]{1,0:T(8,128)(2,1)} copy(bf16[768,4736]{0,1:T(8,128)(2,1)} %pad_dynamic-update-slice_fusion) | data formatting | bytes 14548992
  480.0 5.2 convolution_add_fusion
  495.7 16.2 %reduce-scatter.15.cloned.1.call-done = bf16[24,1536]{1,0:T(8,128)(2,1)} async-done(((bf16[768,1536]{1,0:T(8,128)(2,1)}), bf16[24,1536]{1,0:T(8,128)(2,1)}) %reduce-scatter.15.cloned.1.call-update) | async-done | bytes 73744
  514.6 54.0 %reduce-scatter.9.cloned.1.call-done = bf16[96,3072]{1,0:T(8,128)(2,1)} async-done(((bf16[768,3072]{1,0:T(8,128)(2,1)}), bf16[96,3072]{1,0:T(8,128)(2,1)}) %reduce-scatter.9.cloned.1.call-update) | async-done | bytes 589840 | tf_op jit(solution)/shard_map/reduce_scatter | solution.py:163
  570.8 55.2 %reduce-scatter.11.cloned.1.call-done = bf16[384,768]{1,0:T(8,128)(2,1)} async-done(((bf16[3072,768]{1,0:T(8,128)(2,1)}), bf16[384,768]{1,0:T(8,128)(2,1)}) %reduce-scatter.11.cloned.1.call-update) | async-done | bytes 589840 | tf_op jit(solution)/shard_map/reduce_scatter | solution.py:163
  628.1 68.3 %reduce-scatter.13.cloned.1.call-done = bf16[96,4736]{1,0:T(8,128)(2,1)} async-done(((bf16[768,4736]{1,0:T(8,128)(2,1)}), bf16[96,4736]{1,0:T(8,128)(2,1)}) %reduce-scatter.13.cloned.1.call-update) | async-done | bytes 909328
  (255 shorter events, 220.2 us)
Async XLA Ops:
  7.2 69.5 %copy-start = (bf16[4,320,768]{2,1,0:T(8,128)(2,1)S(1)}, bf16[4,320,768]{2,1,0:T(8,128)(2,1)}, u32[]{:S(2)}) copy-start(bf16[4,320,768]{2,1,0:T(8,128)(2,1)} %param.21) | copy-start | bytes 5898244
  7.2 6.7 copy-start.35
  7.2 69.5 %all-gather.4.cloned.1.call-start = ((), (), s32[]{:S(2)}) async-start(), calls=%async_computation.4 | async-start | bytes 10616832 | tf_op jit(solution)/shard_map/all_gather | solution.py:112
  15.0 217.1 %all-reduce.4.cloned.1.call-start = ((), (), s32[]{:S(2)}) async-start(), calls=%async_computation.5 | async-start | bytes 1572864 | tf_op jit(solution)/shard_map/psum | solution.py:146
  16.3 82.9 %copy-start.33 = (bf16[400,768]{1,0:T(8,128)(2,1)}, bf16[400,768]{1,0:T(8,128)(2,1)S(1)}, u32[]{:S(2)}) copy-start(bf16[400,768]{1,0:T(8,128)(2,1)S(1)} %reshape.213) | copy-start | bytes 1843204
  99.2 8.4 %copy-start.14 = (bf16[4,100,12,64]{1,3,2,0:T(8,128)(2,1)}, bf16[4,100,12,64]{1,3,2,0:T(8,128)(2,1)S(1)}, u32[]{:S(2)}) copy-start(bf16[4,100,12,64]{1,3,2,0:T(8,128)(2,1)S(1)} %copy.221) | copy-start | bytes 1843204
  189.9 82.4 %all-gather.6.cloned.1.call-start = ((), (), s32[]{:S(2)}) async-start(), calls=%async_computation.6 | async-start | bytes 5308416 | tf_op jit(solution)/shard_map/all_gather | solution.py:113
  190.6 122.4 %all-gather.8.cloned.1.call-start = ((), (), s32[]{:S(2)}) async-start(), calls=%async_computation.7 | async-start | bytes 5308416 | tf_op jit(solution)/shard_map/all_gather | solution.py:114
  191.2 219.6 %all-reduce.6.cloned.1.call-start = ((), (), s32[]{:S(2)}) async-start(), calls=%async_computation.8 | async-start | bytes 1572864 | tf_op jit(solution)/shard_map/psum | solution.py:178
  196.0 76.3 %copy-start.38 = (f32[768]{0:T(1024)S(1)}, f32[768]{0:T(1024)}, u32[]{:S(2)}) copy-start(f32[768]{0:T(1024)} %param.35) | copy-start | bytes 9220
  196.0 76.3 %copy-start.43 = (f32[768]{0:T(1024)S(1)}, f32[768]{0:T(1024)}, u32[]{:S(2)}) copy-start(f32[768]{0:T(1024)} %param.36) | copy-start | bytes 9220
  313.0 10.7 %copy-start.46 = (f32[400,3072]{1,0:T(8,128)S(1)}, f32[400,3072]{1,0:T(8,128)}, u32[]{:S(2)}) copy-start(f32[400,3072]{1,0:T(8,128)} %fusion.79) | copy-start | bytes 14745604
  322.2 7.2 slice-start.2
  323.7 5.6 copy-start.29
  324.4 5.0 slice-start.3
  346.7 6.7 copy-start.1
  364.5 147.4 %reduce-scatter.15.cloned.1.call-start = ((), (), s32[]{:S(2)}) async-start(), calls=%async_computation.12 | async-start | bytes 2433024
  395.0 173.6 %reduce-scatter.9.cloned.1.call-start = ((), (), s32[]{:S(2)}) async-start(), calls=%async_computation.9 | async-start | bytes 5308416 | tf_op jit(solution)/shard_map/reduce_scatter | solution.py:163
  402.1 223.9 %reduce-scatter.11.cloned.1.call-start = ((), (), s32[]{:S(2)}) async-start(), calls=%async_computation.10 | async-start | bytes 5308416 | tf_op jit(solution)/shard_map/reduce_scatter | solution.py:163
  410.4 286.1 %reduce-scatter.13.cloned.1.call-start = ((), (), s32[]{:S(2)}) async-start(), calls=%async_computation.11 | async-start | bytes 8183808
  480.0 5.2 copy-start.17
  701.7 5.7 copy-start.27
  701.7 6.6 copy-start.26
  701.7 7.5 %copy-start.25 = (f32[96,768]{0,1:T(8,128)S(1)}, f32[96,768]{0,1:T(8,128)}, u32[]{:S(2)}) copy-start(f32[96,768]{0,1:T(8,128)} %get-tuple-element.132) | copy-start | bytes 884740
  (37 other events, 97.3 us)
Sparse Core Ops, SparseCore 0:
  15.1 61.5 all-gather.3
  190.0 42.0 all-reduce.3
  234.0 38.2 all-gather.5
  274.0 38.9 all-gather.7
  364.6 43.6 all-reduce.5
  413.5 98.3 reduce-scatter.14
  515.7 52.8 reduce-scatter.8
  572.1 53.8 reduce-scatter.10
  629.8 66.6 reduce-scatter.12
where the time goes:
time: 723 us; the launch traced here: 718 us
  waiting for transfers between devices  361 us (50%)
  matrix products  145 us (20%)
  local copies, waits for them, and re-layouts  141 us (20%)
  blocking collectives  34.8 us (5%)
  other arithmetic  20.4 us (3%)
  between operations  15 us (2%)
    reduce_scatter x2, waiting for transfers between devices, scattered(): lax.psum_scatter(part, axes, scatter_dimension=0, tiled=True).astype(WIDE)  109 us
    dot_general x30, matrix products, mm(): return lax.dot_general(a, b, (dims, ((), ())), preferred_element_type=WIDE)  102 us
    unnamed x11, waiting for transfers between devices  85.9 us
    all_gather x1, waiting for transfers between devices, on_device(): packed = lax.all_gather(jnp.stack(squares), 'dp', axis=1, tiled=True)  60.3 us
    unnamed x127, local copies, waits for them, and re-layouts  47.8 us
    reshape x13, local copies, waits for them, and re-layouts, heads_of(): return values.reshape(images, rows // images, H, width // H)  38.3 us
    psum x1, waiting for transfers between devices, on_device(): lax.psum(joined(mix(cross_probs.astype(LOW), cross_v)).astype(LOW), 'mem')  36.2 us
    all_gather x1, waiting for transfers between devices, on_device(): expand_full = lax.all_gather(expand_weight, 'dp', axis=0, tiled=True)  36.1 us
  transfers between devices with their start and end apart: 9, of which 8 were waited for; matrix products, arithmetic and copies ran while one was open for 21% of the time, Pallas kernels for 0%

commit v1 on v0

--- a/solution.py
+++ b/solution.py
@@ -2,6 +2,7 @@
 import jax.numpy as jnp
 from jax import lax
 from jax.sharding import PartitionSpec as P
+from jax.lax import axis_index, axis_size, ppermute
 
 H = 12
 LOW = jnp.bfloat16
@@ -110,7 +111,28 @@
         cross_out,
     )
     packed = lax.all_gather(jnp.stack(squares), "dp", axis=1, tiled=True)
-    expand_full = lax.all_gather(expand_weight, "dp", axis=0, tiled=True)
+    y_new = axis_size("dp")
+    tile_out, e_next, o_now = (y_new, axis_index("dp"), expand_weight.shape[0])
+    all_rows = [(no, (no + 1) % tile_out) for no in range(tile_out)]
+    frames = [(no, (no - 1) % tile_out) for no in range(tile_out)]
+    expand_full = jnp.zeros(
+        (*expand_weight.shape[:0], tile_out * o_now, *expand_weight.shape[1:]), expand_weight.dtype
+    )
+    expand_full = lax.dynamic_update_slice_in_dim(
+        expand_full, expand_weight, e_next * o_now, axis=0
+    )
+    met_up = t1 = expand_weight
+    w_next = tile_out // 2
+    for idx in range(1, w_next + 1):
+        met_up = ppermute(met_up, axis_name="dp", perm=all_rows)
+        expand_full = lax.dynamic_update_slice_in_dim(
+            expand_full, met_up, (e_next - idx) % tile_out * o_now, axis=0
+        )
+        if idx < tile_out - w_next:
+            t1 = ppermute(t1, axis_name="dp", perm=frames)
+            expand_full = lax.dynamic_update_slice_in_dim(
+                expand_full, t1, (e_next + idx) % tile_out * o_now, axis=0
+            )
     contract_full = lax.all_gather(contract_weight, "dp", axis=0, tiled=True)
     query_full, key_full, value_full, out_full, cquery_full, ckey_full, cvalue_full, cout_full = (
         packed

time: 723 us -> 690 us (0.954)
  waiting for transfers between devices: 361 us -> 304 us
  local copies, waits for them, and re-layouts: 141 us -> 154 us
  starting transfers between devices: 0.94 us -> 8.87 us
    ppermute x0 -> x7, waiting for transfers between devices: none -> 42.2 us  [the longest x4 42.2 us: on_device(): met_up = ppermute(met_up, axis_name='dp', perm=all_rows)]
    psum x1, waiting for transfers between devices: 36.2 us -> 0.01 us  [on_device(): lax.psum(joined(mix(cross_probs.astype(LOW), cross_v)).astype(LOW), 'mem')]
    all_gather x1 -> x0, waiting for transfers between devices: 36.1 us -> none  [on_device(): expand_full = lax.all_gather(expand_weight, 'dp', axis=0, tiled=True)]
    all_gather x1, waiting for transfers between devices: 33.5 us -> 7.09 us  [on_device(): contract_full = lax.all_gather(contract_weight, 'dp', axis=0, tiled=True)]
    dynamic_update_slice x0 -> x8, local copies, waits for them, and re-layouts: none -> 8.98 us  [the longest x4 4.52 us: on_device(): lax.dynamic_update_slice_in_dim(expand_full, met_up, (e_next - idx) % til...]
    ppermute x0 -> x7, starting transfers between devices: none -> 8.37 us  [the longest x3 7.91 us: on_device(): t1 = ppermute(t1, axis_name='dp', perm=frames)]
    unnamed x127 -> x131, local copies, waits for them, and re-layouts: 47.8 us -> 49.1 us
    unnamed x11 -> x10, waiting for transfers between devices: 85.9 us -> 85.3 us
  transfers between devices with their start and end apart: 9 -> 15, of which waited for: 8 -> 10; matrix products, arithmetic and copies ran while one was open for 21% -> 24% of each run, Pallas kernels for 0% -> 0%
where the time goes in v1:
time: 690 us; the launch traced here: 685 us
  waiting for transfers between devices  304 us (44%)
  local copies, waits for them, and re-layouts  154 us (22%)
  matrix products  148 us (21%)
  blocking collectives  34.8 us (5%)
  other arithmetic  20.3 us (3%)
  between operations  15.3 us (2%)
  starting transfers between devices  8.87 us (1%)
    reduce_scatter x2, waiting for transfers between devices, scattered(): lax.psum_scatter(part, axes, scatter_dimension=0, tiled=True).astype(WIDE)  109 us
    dot_general x30, matrix products, mm(): return lax.dot_general(a, b, (dims, ((), ())), preferred_element_type=WIDE)  106 us
    unnamed x10, waiting for transfers between devices  85.3 us
    all_gather x1, waiting for transfers between devices, on_device(): packed = lax.all_gather(jnp.stack(squares), 'dp', axis=1, tiled=True)  60.3 us
    unnamed x131, local copies, waits for them, and re-layouts  49.1 us
    ppermute x4, waiting for transfers between devices, on_device(): met_up = ppermute(met_up, axis_name='dp', perm=all_rows)  42.2 us
    reshape x13, local copies, waits for them, and re-layouts, heads_of(): return values.reshape(images, rows // images, H, width // H)  38.3 us
    pmax x1, blocking collectives, on_device(): top = lax.pmax(jnp.max(cross_raw, axis=-1, keepdims=True), 'mem')  19 us
  transfers between devices with their start and end apart: 15, of which 10 were waited for; matrix products, arithmetic and copies ran while one was open for 24% of the time, Pallas kernels for 0%

profile of v1, /device:TPU:0, one launch (start us, length us, event | category | flops | bytes accessed | tf_op | source)
XLA Modules:
  0.0 685.5 jit_solution(7074112221354108882)
XLA Ops:
  16.4 60.3 %all-gather.3.cloned.1.call-done = bf16[8,768,768]{2,1,0:T(8,128)(2,1)} async-done(((bf16[8,96,768]{2,1,0:T(8,128)(2,1)}), bf16[8,768,768]{2,1,0:T(8,128)(2,1)}) %all-gather.3.cloned.1.call-update) | async-done | bytes 9437200 | tf_op jit(solution)/shard_map/all_gather | solution.py:113
  81.0 5.3 reshape.218
  129.7 5.1 reshape.220
  134.8 6.4 fusion.1
  141.2 19.0 %pmax.7 = f32[4,12,100]{2,1,0:T(8,128)S(1)} all-reduce(f32[4,12,100]{2,1,0:T(8,128)S(1)} %get-tuple-element.144), channel_id=1, replica_groups=mesh['dp'=8,'mem'=4] {'mem'}, use_global_device_ids=true, to_apply=%region_5.6 | all-reduce | flops 4800 | bytes 38400 | tf_op jit(solution)/shard_map/pmax | solution.py:164
  164.7 15.9 %psum.21 = f32[4,12,100]{2,1,0:T(8,128)S(1)} all-reduce(f32[4,12,100]{2,1,0:T(8,128)S(1)} %fusion.3), channel_id=1, replica_groups=mesh['dp'=8,'mem'=4] {'mem'}, use_global_device_ids=true, to_apply=%region_7.8 | all-reduce | flops 4800 | bytes 38400 | tf_op jit(solution)/shard_map/psum | solution.py:166
  181.1 5.3 fusion.44
  201.8 5.5 collective-permute-done
  213.7 10.0 %collective-permute-done.2 = bf16[96,3072]{1,0:T(8,128)(2,1)S(1)} collective-permute-done((bf16[96,3072]{1,0:T(8,128)(2,1)}, bf16[96,3072]{1,0:T(8,128)(2,1)S(1)}, u32[]{:S(2)}, u32[]{:S(2)}) %collective-permute-start.2) | collective-permute-done | bytes 589856 | tf_op jit(solution)/shard_map/ppermute | solution.py:127
  228.1 11.9 %collective-permute-done.4 = bf16[96,3072]{1,0:T(8,128)(2,1)S(1)} collective-permute-done((bf16[96,3072]{1,0:T(8,128)(2,1)S(1)}, bf16[96,3072]{1,0:T(8,128)(2,1)S(1)}, u32[]{:S(2)}, u32[]{:S(2)}) %collective-permute-start.4) | collective-permute-done | bytes 589856 | tf_op jit(solution)/shard_map/ppermute | solution.py:127
  242.1 14.8 %collective-permute-done.6 = bf16[96,3072]{1,0:T(8,128)(2,1)S(1)} collective-permute-done((bf16[96,3072]{1,0:T(8,128)(2,1)S(1)}, bf16[96,3072]{1,0:T(8,128)(2,1)S(1)}, u32[]{:S(2)}, u32[]{:S(2)}) %collective-permute-start.6) | collective-permute-done | bytes 589856 | tf_op jit(solution)/shard_map/ppermute | solution.py:127
  261.9 6.8 fusion.79
  268.7 7.1 %all-gather.5.cloned.1.call-done = bf16[3072,768]{1,0:T(8,128)(2,1)} async-done(((bf16[384,768]{1,0:T(8,128)(2,1)}), bf16[3072,768]{1,0:T(8,128)(2,1)}) %all-gather.5.cloned.1.call-update) | async-done | bytes 4718608 | tf_op jit(solution)/shard_map/all_gather | solution.py:136
  275.8 7.3 %fusion.92 = (f32[400]{0:T(512)S(1)}, f32[400,768]{1,0:T(8,128)S(1)}) fusion(bf16[3072,768]{1,0:T(8,128)(2,1)} %all-gather.5.cloned.1.call-done, f32[400,3072]{1,0:T(8,128)} %fusion.79, f32[768]{0:T(1024)S(1)} %copy-done.46, f32[768]{0:T(1024)S(1)} %copy-done.41, f32[400]{0:T(512)S(1)} %add_rsqrt_fusion.1, f32[400,768]{1,0:T(8,128)} %copy-done.10, ...), kind=kOutput, calls=%fused_computation.180 | convolution fusion | flops 1900338816 | bytes 12102336 | tf_op jit(solution)/shard_map/dot_general | solution.py:13
  293.1 5.8 multiply_reduce_fusion.4
  313.8 6.7 multiply_convert_fusion
  362.1 7.1 %convolution_convert_fusion.1 = bf16[768,3072]{1,0:T(8,128)(2,1)} fusion(bf16[400,3072]{1,0:T(8,128)(2,1)} %copy-done.51, f32[400,768]{1,0:T(8,128)} %copy-done.10, f32[768]{0:T(1024)S(1)} %copy-done.46, f32[768]{0:T(1024)S(1)} %copy-done.41, f32[400]{0:T(512)S(1)} %add_rsqrt_fusion.1, f32[400]{0:T(512)S(1)} %broadcast_multiply_fusion.7), kind=kOutput, calls=%fused_computation.10 | convolution fusion | flops 1891332096 | bytes 8414336 | tf_op jit(solution)/shard_map/dot_general | solution.py:13
  369.4 8.0 %convolution_convert_fusion = bf16[3072,768]{1,0:T(8,128)(2,1)} fusion(f32[400,768]{1,0:T(8,128)} %copy-done.29, f32[400,3072]{1,0:T(8,128)} %fusion.79), kind=kOutput, calls=%fused_computation.9 | convolution fusion | flops 1901162496 | bytes 10862592 | tf_op jit(solution)/shard_map/dot_general | solution.py:13
  428.3 10.1 %copy.272 = bf16[768,4736]{1,0:T(8,128)(2,1)} copy(bf16[768,4736]{0,1:T(8,128)(2,1)} %pad_dynamic-update-slice_fusion) | data formatting | bytes 14548992
  447.1 5.2 convolution_add_fusion
  462.8 16.2 %reduce-scatter.15.cloned.1.call-done = bf16[24,1536]{1,0:T(8,128)(2,1)} async-done(((bf16[768,1536]{1,0:T(8,128)(2,1)}), bf16[24,1536]{1,0:T(8,128)(2,1)}) %reduce-scatter.15.cloned.1.call-update) | async-done | bytes 73744
  481.6 53.9 %reduce-scatter.9.cloned.1.call-done = bf16[96,3072]{1,0:T(8,128)(2,1)} async-done(((bf16[768,3072]{1,0:T(8,128)(2,1)}), bf16[96,3072]{1,0:T(8,128)(2,1)}) %reduce-scatter.9.cloned.1.call-update) | async-done | bytes 589840 | tf_op jit(solution)/shard_map/reduce_scatter | solution.py:185
  537.7 55.2 %reduce-scatter.11.cloned.1.call-done = bf16[384,768]{1,0:T(8,128)(2,1)} async-done(((bf16[3072,768]{1,0:T(8,128)(2,1)}), bf16[384,768]{1,0:T(8,128)(2,1)}) %reduce-scatter.11.cloned.1.call-update) | async-done | bytes 589840 | tf_op jit(solution)/shard_map/reduce_scatter | solution.py:185
  595.0 68.3 %reduce-scatter.13.cloned.1.call-done = bf16[96,4736]{1,0:T(8,128)(2,1)} async-done(((bf16[768,4736]{1,0:T(8,128)(2,1)}), bf16[96,4736]{1,0:T(8,128)(2,1)}) %reduce-scatter.13.cloned.1.call-update) | async-done | bytes 909328
  (278 shorter events, 253.2 us)
Async XLA Ops:
  7.2 69.5 %copy-start = (bf16[4,320,768]{2,1,0:T(8,128)(2,1)S(1)}, bf16[4,320,768]{2,1,0:T(8,128)(2,1)}, u32[]{:S(2)}) copy-start(bf16[4,320,768]{2,1,0:T(8,128)(2,1)} %param.21) | copy-start | bytes 5898244
  7.2 6.7 copy-start.36
  7.2 69.5 %all-gather.3.cloned.1.call-start = ((), (), s32[]{:S(2)}) async-start(), calls=%async_computation.4 | async-start | bytes 10616832 | tf_op jit(solution)/shard_map/all_gather | solution.py:113
  15.0 242.8 %all-reduce.4.cloned.1.call-start = ((), (), s32[]{:S(2)}) async-start(), calls=%async_computation.5 | async-start | bytes 1572864 | tf_op jit(solution)/shard_map/psum | solution.py:168
  16.3 82.9 %copy-start.33 = (bf16[400,768]{1,0:T(8,128)(2,1)}, bf16[400,768]{1,0:T(8,128)(2,1)S(1)}, u32[]{:S(2)}) copy-start(bf16[400,768]{1,0:T(8,128)(2,1)S(1)} %reshape.213) | copy-start | bytes 1843204
  99.2 8.4 %copy-start.14 = (bf16[4,100,12,64]{1,3,2,0:T(8,128)(2,1)}, bf16[4,100,12,64]{1,3,2,0:T(8,128)(2,1)S(1)}, u32[]{:S(2)}) copy-start(bf16[4,100,12,64]{1,3,2,0:T(8,128)(2,1)S(1)} %copy.221) | copy-start | bytes 1843204
  186.4 7.5 %copy-start.3 = (bf16[4,100,768]{2,0,1:T(4,128)(2,1)S(1)}, bf16[4,100,768]{2,0,1:T(4,128)(2,1)}, u32[]{:S(2)}) copy-start(bf16[4,100,768]{2,0,1:T(4,128)(2,1)} %param.39) | copy-start | bytes 1843204
  186.4 7.5 %copy-start.37 = (f32[768]{0:T(1024)S(1)}, f32[768]{0:T(1024)}, u32[]{:S(2)}) copy-start(f32[768]{0:T(1024)} %param.37) | copy-start | bytes 9220
  190.4 85.4 %all-gather.5.cloned.1.call-start = ((), (), s32[]{:S(2)}) async-start(), calls=%async_computation.6 | async-start | bytes 5308416 | tf_op jit(solution)/shard_map/all_gather | solution.py:136
  191.1 186.7 %all-reduce.6.cloned.1.call-start = ((), (), s32[]{:S(2)}) async-start(), calls=%async_computation.7 | async-start | bytes 1572864 | tf_op jit(solution)/shard_map/psum | solution.py:200
  191.2 16.1 %collective-permute-start = (bf16[96,3072]{1,0:T(8,128)(2,1)}, bf16[96,3072]{1,0:T(8,128)(2,1)}, u32[]{:S(2)}, u32[]{:S(2)}) collective-permute-start(bf16[96,3072]{1,0:T(8,128)(2,1)} %param.31), channel_id=1, source_target_pairs={{0,4},{4,8},{8,12},{12,16},{16,20},{20,24},{24,28},{28,0},{1,5},{5... | collective-permute-start | bytes 1769480 | tf_op jit(solution)/shard_map/ppermute | solution.py:127
  191.2 16.0 %collective-permute-start.1 = (bf16[96,3072]{1,0:T(8,128)(2,1)}, bf16[96,3072]{1,0:T(8,128)(2,1)}, u32[]{:S(2)}, u32[]{:S(2)}) collective-permute-start(bf16[96,3072]{1,0:T(8,128)(2,1)} %param.31), channel_id=1, source_target_pairs={{0,28},{4,0},{8,4},{12,8},{16,12},{20,16},{24,20},{28,24},{1,29},{... | collective-permute-start | bytes 1769480 | tf_op jit(solution)/shard_map/ppermute | solution.py:132
  207.2 16.5 %collective-permute-start.2 = (bf16[96,3072]{1,0:T(8,128)(2,1)}, bf16[96,3072]{1,0:T(8,128)(2,1)S(1)}, u32[]{:S(2)}, u32[]{:S(2)}) collective-permute-start(bf16[96,3072]{1,0:T(8,128)(2,1)} %collective-permute-done), channel_id=1, source_target_pairs={{0,4},{4,8},{8,12},{12,16},{16,20},{20,24},{24,28},{28,0},{1,5},{5... | collective-permute-start | bytes 1769480 | tf_op jit(solution)/shard_map/ppermute | solution.py:127
  207.2 16.5 %collective-permute-start.3 = (bf16[96,3072]{1,0:T(8,128)(2,1)}, bf16[96,3072]{1,0:T(8,128)(2,1)S(1)}, u32[]{:S(2)}, u32[]{:S(2)}) collective-permute-start(bf16[96,3072]{1,0:T(8,128)(2,1)} %collective-permute-done.1), channel_id=1, source_target_pairs={{0,28},{4,0},{8,4},{12,8},{16,12},{20,16},{24,20},{28,24},{1,29},{... | collective-permute-start | bytes 1769480 | tf_op jit(solution)/shard_map/ppermute | solution.py:132
  223.7 16.3 %collective-permute-start.4 = (bf16[96,3072]{1,0:T(8,128)(2,1)S(1)}, bf16[96,3072]{1,0:T(8,128)(2,1)S(1)}, u32[]{:S(2)}, u32[]{:S(2)}) collective-permute-start(bf16[96,3072]{1,0:T(8,128)(2,1)S(1)} %collective-permute-done.2), channel_id=1, source_target_pairs={{0,4},{4,8},{8,12},{12,16},{16,20},{20,24},{24,28},{28,0},{1,5},{5... | collective-permute-start | bytes 1769480 | tf_op jit(solution)/shard_map/ppermute | solution.py:127
  223.8 17.5 %collective-permute-start.5 = (bf16[96,3072]{1,0:T(8,128)(2,1)S(1)}, bf16[96,3072]{1,0:T(8,128)(2,1)S(1)}, u32[]{:S(2)}, u32[]{:S(2)}) collective-permute-start(bf16[96,3072]{1,0:T(8,128)(2,1)S(1)} %collective-permute-done.3), channel_id=1, source_target_pairs={{0,28},{4,0},{8,4},{12,8},{16,12},{20,16},{24,20},{28,24},{1,29},{... | collective-permute-start | bytes 1769480 | tf_op jit(solution)/shard_map/ppermute | solution.py:132
  228.1 29.7 %copy-start.48 = (f32[768]{0:T(1024)S(1)}, f32[768]{0:T(1024)}, u32[]{:S(2)}) copy-start(f32[768]{0:T(1024)} %param.34) | copy-start | bytes 9220
  240.0 16.9 %collective-permute-start.6 = (bf16[96,3072]{1,0:T(8,128)(2,1)S(1)}, bf16[96,3072]{1,0:T(8,128)(2,1)S(1)}, u32[]{:S(2)}, u32[]{:S(2)}) collective-permute-start(bf16[96,3072]{1,0:T(8,128)(2,1)S(1)} %collective-permute-done.4), channel_id=1, source_target_pairs={{0,4},{4,8},{8,12},{12,16},{16,20},{20,24},{24,28},{28,0},{1,5},{5... | collective-permute-start | bytes 1769480 | tf_op jit(solution)/shard_map/ppermute | solution.py:127
  275.8 10.7 %copy-start.50 = (f32[400,3072]{1,0:T(8,128)S(1)}, f32[400,3072]{1,0:T(8,128)}, u32[]{:S(2)}) copy-start(f32[400,3072]{1,0:T(8,128)} %fusion.79) | copy-start | bytes 14745604
  331.5 147.4 %reduce-scatter.15.cloned.1.call-start = ((), (), s32[]{:S(2)}) async-start(), calls=%async_computation.11 | async-start | bytes 2433024
  362.0 173.5 %reduce-scatter.9.cloned.1.call-start = ((), (), s32[]{:S(2)}) async-start(), calls=%async_computation.8 | async-start | bytes 5308416 | tf_op jit(solution)/shard_map/reduce_scatter | solution.py:185
  369.2 223.7 %reduce-scatter.11.cloned.1.call-start = ((), (), s32[]{:S(2)}) async-start(), calls=%async_computation.9 | async-start | bytes 5308416 | tf_op jit(solution)/shard_map/reduce_scatter | solution.py:185
  377.4 285.9 %reduce-scatter.13.cloned.1.call-start = ((), (), s32[]{:S(2)}) async-start(), calls=%async_computation.10 | async-start | bytes 8183808
  668.6 7.5 %copy-start.25 = (f32[96,768]{0,1:T(8,128)S(1)}, f32[96,768]{0,1:T(8,128)}, u32[]{:S(2)}) copy-start(f32[96,768]{0,1:T(8,128)} %get-tuple-element.132) | copy-start | bytes 884740
  (45 other events, 140.5 us)
Sparse Core Ops, SparseCore 0:
  15.1 61.5 all-gather.2
  190.5 42.0 all-reduce.3
  234.5 41.1 all-gather.4
  331.7 43.6 all-reduce.5
  380.5 98.3 reduce-scatter.14
  482.6 52.8 reduce-scatter.8
  539.0 53.8 reduce-scatter.10
  596.7 66.6 reduce-scatter.12
